TPU v7x, 128 devices: a whole 4x4x4 slice. The times are simulated.
128 devices in a mesh: fsdp: 16 (over z, y), tensor: 8 (over x, core).
Axes of the slice: x: 4, y: 4, z: 4, core: 2. Of those that a mesh axis runs over, the one named last changes fastest.
Arguments:
- grad_blocks: bfloat16 [2, 16896, 1536], P(None, 'tensor', 'fsdp'), may hold values from -150 to 150
- master_shard: float32 [2, 16896, 1536], P(None, ('fsdp', 'tensor')), may hold values from -6 to 6
- first_moment: float32 [2, 16896, 1536], P(None, ('fsdp', 'tensor')), may hold values from -2 to 2
- second_moment: float32 [2, 16896, 1536], P(None, ('fsdp', 'tensor')), may hold values from 0.05 to 0.5
- average_shard: float32 [2, 16896, 1536], P(None, ('tensor', 'fsdp')), may hold values from -6 to 6
- gain_grads: bfloat16 [2, 3072], P(None, ('fsdp', 'tensor')), may hold values from -24 to 24
- gain_master: float32 [2, 3072], P(None, ('fsdp', 'tensor')), may hold values from 0.5 to 1.5
- gain_first: float32 [2, 3072], P(None, ('fsdp', 'tensor')), may hold values from -2 to 2
- gain_second: float32 [2, 3072], P(None, ('fsdp', 'tensor')), may hold values from 0.05 to 0.5
- gain_average: float32 [2, 3072], P(None, ('fsdp', 'tensor')), may hold values from 0.5 to 1.5
Outputs:
- train_weights: bfloat16 [2, 16896, 1536], P(None, 'tensor', 'fsdp')
- master_next: float32 [2, 16896, 1536], P(None, ('fsdp', 'tensor'))
- first_next: float32 [2, 16896, 1536], P(None, ('fsdp', 'tensor'))
- second_next: float32 [2, 16896, 1536], P(None, ('fsdp', 'tensor'))
- average_next: float32 [2, 16896, 1536], P(None, ('tensor', 'fsdp'))
- gain_weights: bfloat16 [2, 3072], replicated
- master_gains: float32 [2, 3072], P(None, ('fsdp', 'tensor'))
- first_gains: float32 [2, 3072], P(None, ('fsdp', 'tensor'))
- second_gains: float32 [2, 3072], P(None, ('fsdp', 'tensor'))
- average_gains: float32 [2, 3072], P(None, ('fsdp', 'tensor'))
All inputs are finite; a program needn't handle non-finite values.
Results may differ from a plain program's by a relative error of at most 0.001.
Values may be sent and summed in bfloat16 or wider, within the bound.
A program may use at most 128 MiB of HBM per device.

v0:
```python
import jax
import jax.numpy as jnp
from jax import lax
from jax.sharding import PartitionSpec as P

STEP = 20
learn_rate = 0.1
weight_decay = 0.1
beta_first = 0.9
beta_second = 0.95
adam_epsilon = 1e-08
average_decay = 0.9
clip_level = 0.5
mean_epsilon = 1e-06


def adam_step(gradient, master, first_state, second_state, clip_scale):
    clipped = gradient.astype(jnp.float32) * clip_scale
    first_new = beta_first * first_state + (1.0 - beta_first) * clipped
    second_new = beta_second * second_state + (1.0 - beta_second) * clipped * clipped
    first_fix = 1.0 - beta_first**STEP
    second_fix = 1.0 - beta_second**STEP
    direction = (
        first_new / first_fix / (jnp.sqrt(second_new / second_fix) + adam_epsilon)
        + weight_decay * master
    )
    master_new = master - learn_rate * direction
    return (master_new, first_new, second_new)


def on_device(
    grad_blocks,
    master_shard,
    first_moment,
    second_moment,
    average_shard,
    gain_grads,
    gain_master,
    gain_first,
    gain_second,
    gain_average,
):
    fsdp_count = lax.axis_size("fsdp")
    tensor_count = lax.axis_size("tensor")
    group_ratio = fsdp_count // tensor_count
    layer_count, block_rows, block_cols = grad_blocks.shape
    shard_rows = block_rows // fsdp_count
    width_full = block_cols * fsdp_count
    entries = (grad_blocks.size + gain_grads.size) * fsdp_count * tensor_count
    gain_wide = gain_grads.astype(jnp.float32)
    gain_squares = jnp.sum(gain_wide * gain_wide)
    sectioned = grad_blocks.reshape(layer_count, group_ratio, tensor_count, shard_rows, block_cols)
    arrived = lax.all_to_all(
        lax.all_to_all(sectioned, "tensor", split_axis=2, concat_axis=1, tiled=True),
        "fsdp",
        split_axis=1,
        concat_axis=4,
        tiled=True,
    )
    flat_grads = arrived.reshape(layer_count, shard_rows, width_full)
    flat_wide = flat_grads.astype(jnp.float32)
    total_squares = lax.psum(jnp.sum(flat_wide * flat_wide) + gain_squares, ("fsdp", "tensor"))
    clip_scale = jnp.minimum(1.0, clip_level / jnp.sqrt(total_squares / entries + mean_epsilon))
    master_next, first_next, second_next = adam_step(
        flat_grads, master_shard, first_moment, second_moment, clip_scale
    )
    master_gains, first_gains, second_gains = adam_step(
        gain_grads, gain_master, gain_first, gain_second, clip_scale
    )
    average_gains = average_decay * gain_average + (1.0 - average_decay) * master_gains
    outgoing = master_next.reshape(layer_count, 1, 1, shard_rows, width_full)
    home_float = lax.all_to_all(
        lax.all_to_all(
            outgoing.astype(jnp.bfloat16), "fsdp", split_axis=4, concat_axis=1, tiled=True
        ),
        "tensor",
        split_axis=1,
        concat_axis=2,
        tiled=True,
    ).astype(outgoing.dtype)
    train_float = home_float.reshape(layer_count, block_rows, block_cols)
    train_weights = train_float.astype(jnp.bfloat16)
    sorted_rows = train_float.reshape(layer_count, fsdp_count, shard_rows, block_cols)
    average_rows = lax.all_to_all(
        sorted_rows.astype(jnp.bfloat16), "fsdp", split_axis=1, concat_axis=3, tiled=True
    ).astype(sorted_rows.dtype)
    average_layout = average_rows.reshape(layer_count, shard_rows, width_full)
    average_next = average_decay * average_shard + (1.0 - average_decay) * average_layout
    gain_weights = lax.all_gather(
        master_gains.astype(jnp.bfloat16), ("fsdp", "tensor"), axis=1, tiled=True
    )
    return (
        train_weights,
        master_next,
        first_next,
        second_next,
        average_next,
        gain_weights,
        master_gains,
        first_gains,
        second_gains,
        average_gains,
    )


def solution(mesh):
    placed = (
        P(None, "tensor", "fsdp"),
        P(None, ("fsdp", "tensor"), None),
        P(None, ("fsdp", "tensor"), None),
        P(None, ("fsdp", "tensor"), None),
        P(None, ("tensor", "fsdp"), None),
        P(None, ("fsdp", "tensor")),
        P(None, ("fsdp", "tensor")),
        P(None, ("fsdp", "tensor")),
        P(None, ("fsdp", "tensor")),
        P(None, ("fsdp", "tensor")),
    )
    return jax.shard_map(
        on_device,
        mesh=mesh,
        in_specs=placed,
        out_specs=(
            P(None, "tensor", "fsdp"),
            P(None, ("fsdp", "tensor"), None),
            P(None, ("fsdp", "tensor"), None),
            P(None, ("fsdp", "tensor"), None),
            P(None, ("tensor", "fsdp"), None),
            P(),
            P(None, ("fsdp", "tensor")),
            P(None, ("fsdp", "tensor")),
            P(None, ("fsdp", "tensor")),
            P(None, ("fsdp", "tensor")),
        ),
        check_vma=False,
    )
```

profile of v0, /device:TPU:1, one launch (start us, length us, event | category | flops | bytes accessed | tf_op | source)
XLA Modules:
  0.0 253.8 jit_solution(17145453859018370600)
XLA Ops:
  0.6 5.4 %reshape.52 = bf16[2,2,8,132,96]{3,2,1,4,0:T(8,128)(2,1)S(1)} reshape(bf16[2,2112,96]{1,2,0:T(8,128)(2,1)} %param.10) | data formatting | bytes 1622016 | tf_op jit(solution)/shard_map/reshape | solution.py:52
  6.0 2.1 copy.92
  8.1 21.5 %all_to_all.75 = bf16[2,2,8,132,96]{4,1,3,0,2:T(2,128)(2,1)S(1)} all-to-all(bf16[2,2,8,132,96]{4,1,3,0,2:T(2,128)(2,1)S(1)} %copy.92), channel_id=1, replica_groups=mesh['fsdp'=16,'tensor'=8] {'tensor'}, dimensions={2} | all-to-all | bytes 1622016 | tf_op jit(solution)/shard_map/all_to_all | solution.py:54
  29.6 0.7 copy.93
  30.3 0.0 copy-start.6
  30.4 2.1 copy.94
  32.5 7.8 %all-to-all-start.1 = ((bf16[2,16,1,132,96]{4,0,3,2,1:T(2,128)(2,1)}), bf16[2,16,1,132,96]{4,0,3,2,1:T(2,128)(2,1)S(1)}, u32[]{:S(2)}, u32[]{:S(2)}) async-start(bf16[2,16,1,132,96]{4,0,3,2,1:T(2,128)(2,1)} %copy.94), calls=%async_computation.1 | async-start | bytes 2162688 | tf_op jit(solution)/shard_map/all_to_all | solution.py:53
  40.2 0.0 copy-done.6
  40.2 0.6 fusion.7
  40.8 15.9 %all-to-all-done.1 = bf16[2,16,1,132,96]{4,0,3,2,1:T(2,128)(2,1)S(1)} async-done(((bf16[2,16,1,132,96]{4,0,3,2,1:T(2,128)(2,1)}), bf16[2,16,1,132,96]{4,0,3,2,1:T(2,128)(2,1)S(1)}, u32[]{:S(2)}, u32[]{:S(2)}) %all-to-all-start.1) | async-done | bytes 811040 | tf_op jit(solution)/shard_map/all_to_all | solution.py:53
  56.7 2.8 %fusion = f32[]{:T(128)} fusion(bf16[2,16,1,132,96]{4,0,3,2,1:T(2,128)(2,1)S(1)} %all-to-all-done.1), kind=kLoop, calls=%fused_computation.3 | loop fusion | flops 1216511 | bytes 811012 | tf_op jit(solution)/shard_map/reduce_sum | solution.py:62
  60.8 64.4 %psum.7 = f32[]{:T(128)} all-reduce(f32[]{:T(128)S(6)} %add.44), channel_id=1, replica_groups=mesh['fsdp'=16,'tensor'=8] {'fsdp','tensor'}, use_global_device_ids=true, to_apply=%region_2.0 | all-reduce | flops 1 | bytes 8 | tf_op jit(solution)/shard_map/psum | solution.py:62
  125.9 0.7 fusion.1
  126.7 0.4 copy.95
  127.1 2.3 mul.112
  129.4 6.5 %convert_bitcast_fusion = (bf16[2,1,1,132,1536]{4,3,0,2,1:T(8,128)(2,1)}, f32[2,132,1536]{2,1,0:T(8,128)}, f32[2,132,1536]{2,1,0:T(8,128)}, f32[2,132,1536]{2,1,0:T(8,128)S(1)}) fusion(f32[2,132,1536]{2,0,1:T(2,128)} %param.11, f32[2,132,1536]{2,1,0:T(8,128)} %mul.112, f32[2,132,1536]{2,0,1:T(2,128)} %param.12, f32[2,132,1536]{2,0,1:T(2,128)} %param.13), kind=kLoop, calls=%fused_computation.14 | loop fusion | flops 6488064 | bytes 12165120 | tf_op jit(solution)/shard_map/convert_element_type | solution.py:74
  135.9 3.5 %copy.99 = bf16[2,1,1,132,1536]{3,0,2,1,4:T(2,128)(2,1)S(1)} copy(bf16[2,1,1,132,1536]{4,3,0,2,1:T(8,128)(2,1)} %get-tuple-element.74) | data formatting | bytes 1622016 | tf_op jit(solution)/shard_map/convert_element_type | solution.py:74
  139.5 25.4 %all_to_all.76 = bf16[2,1,1,132,1536]{3,0,2,1,4:T(2,128)(2,1)} all-to-all(bf16[2,1,1,132,1536]{3,0,2,1,4:T(2,128)(2,1)S(1)} %copy.99), channel_id=1, replica_groups=mesh['fsdp'=16,'tensor'=8] {'fsdp'}, dimensions={4} | all-to-all | bytes 1622016 | tf_op jit(solution)/shard_map/all_to_all | solution.py:73
  164.9 3.5 %copy.116 = bf16[2,1,1,132,16,96]{5,4,3,0,2,1:T(8,128)(2,1)S(1)} copy(bf16[2,1,1,132,16,96]{3,0,5,4,2,1:T(2,128)(2,1)} %bitcast.47) | data formatting | bytes 1622016 | tf_op jit(solution)/shard_map/all_to_all | solution.py:73
  168.4 1.1 copy.101
  169.5 20.2 %all_to_all.77 = bf16[2,16,1,132,96]{4,0,3,2,1:T(2,128)(2,1)S(1)} all-to-all(bf16[2,16,1,132,96]{4,0,3,2,1:T(2,128)(2,1)S(1)} %copy.101), channel_id=1, replica_groups=mesh['fsdp'=16,'tensor'=8] {'tensor'}, dimensions={1} | all-to-all | bytes 1622016 | tf_op jit(solution)/shard_map/all_to_all | solution.py:72
  189.7 0.1 copy.102
  189.8 0.1 copy.133
  190.0 2.1 copy.106
  192.1 4.6 %all-to-all-start.4 = ((bf16[2,16,132,96]{3,0,2,1:T(2,128)(2,1)}), bf16[2,16,132,96]{3,0,2,1:T(2,128)(2,1)}, u32[]{:S(2)}, u32[]{:S(2)}) async-start(bf16[2,16,132,96]{3,0,2,1:T(2,128)(2,1)} %copy.106), calls=%async_computation.4 | async-start | bytes 2162688 | tf_op jit(solution)/shard_map/all_to_all | solution.py:84
  196.7 0.0 copy-start
  196.7 4.0 %copy.110 = f32[2,132,1536]{2,0,1:T(2,128)} copy(f32[2,132,1536]{2,1,0:T(8,128)} %get-tuple-element.75) | data formatting | bytes 3244032
  200.7 0.0 copy-done
  200.7 2.4 copy.111
  203.1 0.0 copy-start.1
  203.1 0.0 copy-start.2
  203.1 2.4 copy.112
  205.5 0.0 copy-done.1
  205.5 0.0 copy-done.2
  205.5 0.0 copy-done.3
  205.5 0.0 copy-done.4
  205.5 0.6 multiply_add_fusion
  206.1 31.2 %all-gather = bf16[128,24,2]{1,2,0:T(2,128)(2,1)S(1)} all-gather(bf16[1,24,2]{1,2,0:T(2,128)(2,1)S(1)} %convert_bitcast_fusion.1), channel_id=1, replica_groups=mesh['fsdp'=16,'tensor'=8] {'fsdp','tensor'}, dimensions={0}, use_global_device_ids=true | all-gather | bytes 12384 | tf_op jit(solution)/shard_map/all_gather | solution.py:89
  237.4 0.7 reshape.51
  238.1 3.0 %copy.117 = bf16[2,2,8,1,132,96]{4,2,1,5,0,3:T(8,128)(2,1)S(1)} copy(bf16[2,2,8,1,132,96]{5,1,2,4,0,3:T(2,128)(2,1)S(1)} %bitcast.46) | data formatting | bytes 1622016
  241.1 2.9 %reshape.53 = bf16[2,2112,96]{1,2,0:T(8,128)(2,1)} reshape(bf16[2,2,8,1,132,96]{4,2,1,5,0,3:T(8,128)(2,1)S(1)} %copy.117) | data formatting | bytes 1622016
  244.0 0.0 copy-done.5
  244.0 0.0 all-to-all-done.4
  244.0 2.4 multiply_bitcast_fusion
  246.3 0.4 copy.107
  246.8 2.3 mul.125
  249.1 2.4 fusion.3
  251.4 2.4 copy.113
  (5 shorter events, 0.0 us)
Async XLA Ops:
  30.3 9.9 %copy-start.6 = (bf16[2,24]{1,0:T(2,128)(2,1)S(1)}, bf16[2,24]{1,0:T(2,128)(2,1)}, u32[]{:S(2)}) copy-start(bf16[2,24]{1,0:T(2,128)(2,1)} %param.15) | copy-start | bytes 292
  32.5 24.2 %all-to-all-start.1 = ((bf16[2,16,1,132,96]{4,0,3,2,1:T(2,128)(2,1)}), bf16[2,16,1,132,96]{4,0,3,2,1:T(2,128)(2,1)S(1)}, u32[]{:S(2)}, u32[]{:S(2)}) async-start(bf16[2,16,1,132,96]{4,0,3,2,1:T(2,128)(2,1)} %copy.94), calls=%async_computation.1 | async-start | bytes 2162688 | tf_op jit(solution)/shard_map/all_to_all | solution.py:53
  192.1 51.9 %all-to-all-start.4 = ((bf16[2,16,132,96]{3,0,2,1:T(2,128)(2,1)}), bf16[2,16,132,96]{3,0,2,1:T(2,128)(2,1)}, u32[]{:S(2)}, u32[]{:S(2)}) async-start(bf16[2,16,132,96]{3,0,2,1:T(2,128)(2,1)} %copy.106), calls=%async_computation.4 | async-start | bytes 2162688 | tf_op jit(solution)/shard_map/all_to_all | solution.py:84
  196.7 4.0 %copy-start = (f32[2,132,1536]{2,1,0:T(8,128)S(1)}, f32[2,132,1536]{2,1,0:T(8,128)}, u32[]{:S(2)}) copy-start(f32[2,132,1536]{2,1,0:T(8,128)} %get-tuple-element.76) | copy-start | bytes 4866052
  203.1 2.4 copy-start.1
  203.1 2.4 copy-start.2
  203.1 2.4 copy-start.3
  203.1 2.4 copy-start.4
  206.1 37.9 %copy-start.5 = (f32[2,24]{1,0:T(2,128)}, f32[2,24]{1,0:T(2,128)S(1)}, u32[]{:S(2)}) copy-start(f32[2,24]{1,0:T(2,128)S(1)} %get-tuple-element.71) | copy-start | bytes 580
where the time goes:
time: 255 us; the launch traced here: 254 us
  blocking collectives  163 us (64%)
  local copies, waits for them, and re-layouts  44 us (17%)
  other arithmetic  16 us (6%)
  waiting for transfers between devices  15.9 us (6%)
  starting transfers between devices  12.4 us (5%)
  between operations  2.8 us (1%)
    psum x1, blocking collectives, on_device(): lax.psum(jnp.sum(flat_wide * flat_wide) + gain_squares, ('fsdp', 'tensor'))  64.4 us
    all_gather x1, blocking collectives, on_device(): lax.all_gather(master_gains.astype(jnp.bfloat16), ('fsdp', 'tensor'), axi...  31.2 us
    all_to_all x1, blocking collectives, on_device(): lax.all_to_all(outgoing.astype(jnp.bfloat16), 'fsdp', split_axis=4, conca...  25.4 us
    all_to_all x1, blocking collectives, on_device(): lax.all_to_all(sectioned, 'tensor', split_axis=2, concat_axis=1, tiled=True)  21.5 us
    all_to_all x1, blocking collectives, on_device(): lax.all_to_all(lax.all_to_all(outgoing.astype(jnp.bfloat16), 'fsdp', spli...  20.2 us
    unnamed x21, local copies, waits for them, and re-layouts  17.9 us
    all_to_all x1, waiting for transfers between devices, on_device(): lax.all_to_all(lax.all_to_all(sectioned, 'tensor', split_axis=2, concat_a...  15.9 us
    all_to_all x1, starting transfers between devices, on_device(): lax.all_to_all(lax.all_to_all(sectioned, 'tensor', split_axis=2, concat_a...  7.77 us
  transfers between devices with their start and end apart: 2, of which 1 were waited for; matrix products, arithmetic and copies ran while one was open for 7% of the time, Pallas kernels for 0%

commit v1 on v0

--- a/solution.py
+++ b/solution.py
@@ -86,9 +86,9 @@
     ).astype(sorted_rows.dtype)
     average_layout = average_rows.reshape(layer_count, shard_rows, width_full)
     average_next = average_decay * average_shard + (1.0 - average_decay) * average_layout
-    gain_weights = lax.all_gather(
-        master_gains.astype(jnp.bfloat16), ("fsdp", "tensor"), axis=1, tiled=True
-    )
+    own = master_gains.astype(jnp.bfloat16)
+    repeated = jnp.stack([own] * lax.axis_size(("fsdp", "tensor")))
+    gain_weights = jnp.concatenate(lax.all_to_all(repeated, ("fsdp", "tensor"), 0, 0), axis=1)
     return (
         train_weights,
         master_next,

time: 255 us -> 239 us (0.937)
  blocking collectives: 163 us -> 111 us
  waiting for transfers between devices: 15.9 us -> 37.6 us
  starting transfers between devices: 12.4 us -> 22 us
  local copies, waits for them, and re-layouts: 44 us -> 47.3 us
    all_gather x1 -> x0, blocking collectives: 31.2 us -> none  [on_device(): lax.all_gather(master_gains.astype(jnp.bfloat16), ('fsdp', 'tensor'), axi...]
    all_to_all x0 -> x2, waiting for transfers between devices: none -> 20.9 us  [the longest x1 14.8 us: on_device(): lax.all_to_all(lax.all_to_all(outgoing.astype(jnp.bfloat16), 'fsdp', spli...]
    all_to_all x1 -> x0, blocking collectives: 20.2 us -> none  [on_device(): lax.all_to_all(lax.all_to_all(outgoing.astype(jnp.bfloat16), 'fsdp', spli...]
    all_to_all x0 -> x2, starting transfers between devices: none -> 9.62 us  [the longest x1 5.37 us: on_device(): lax.all_to_all(lax.all_to_all(outgoing.astype(jnp.bfloat16), 'fsdp', spli...]
    unnamed x21 -> x22, local copies, waits for them, and re-layouts: 17.9 us -> 17.4 us
  transfers between devices with their start and end apart: 2 -> 4, of which waited for: 1 -> 4; matrix products, arithmetic and copies ran while one was open for 7% -> 9% of each run, Pallas kernels for 0% -> 0%
where the time goes in v1:
time: 239 us; the launch traced here: 237 us
  blocking collectives  111 us (46%)
  local copies, waits for them, and re-layouts  47.3 us (20%)
  waiting for transfers between devices  37.6 us (16%)
  starting transfers between devices  22 us (9%)
  other arithmetic  16 us (7%)
  between operations  2.84 us (1%)
    psum x1, blocking collectives, on_device(): lax.psum(jnp.sum(flat_wide * flat_wide) + gain_squares, ('fsdp', 'tensor'))  64.4 us
    all_to_all x1, blocking collectives, on_device(): lax.all_to_all(outgoing.astype(jnp.bfloat16), 'fsdp', split_axis=4, conca...  25.4 us
    all_to_all x1, blocking collectives, on_device(): lax.all_to_all(sectioned, 'tensor', split_axis=2, concat_axis=1, tiled=True)  21.5 us
    unnamed x22, local copies, waits for them, and re-layouts  17.4 us
    all_to_all x1, waiting for transfers between devices, on_device(): lax.all_to_all(lax.all_to_all(sectioned, 'tensor', split_axis=2, concat_a...  15.9 us
    all_to_all x1, waiting for transfers between devices, on_device(): lax.all_to_all(lax.all_to_all(outgoing.astype(jnp.bfloat16), 'fsdp', spli...  14.8 us
    all_to_all x1, starting transfers between devices, on_device(): lax.all_to_all(lax.all_to_all(sectioned, 'tensor', split_axis=2, concat_a...  7.77 us
    reshape x2, local copies, waits for them, and re-layouts, on_device(): grad_blocks.reshape(layer_count, group_ratio, tensor_count, shard_rows, b...  7.46 us
  transfers between devices with their start and end apart: 4, of which 4 were waited for; matrix products, arithmetic and copies ran while one was open for 9% of the time, Pallas kernels for 0%

profile of v1, /device:TPU:1, one launch (start us, length us, event | category | flops | bytes accessed | tf_op | source)
XLA Modules:
  0.0 237.1 jit_solution(8874222611382244536)
XLA Ops:
  0.6 5.4 %reshape.60 = bf16[2,2,8,132,96]{3,2,1,4,0:T(8,128)(2,1)S(1)} reshape(bf16[2,2112,96]{1,2,0:T(8,128)(2,1)} %param.10) | data formatting | bytes 1622016 | tf_op jit(solution)/shard_map/reshape | solution.py:52
  6.0 2.1 copy.88
  8.1 21.5 %all_to_all.80 = bf16[2,2,8,132,96]{4,1,3,0,2:T(2,128)(2,1)S(1)} all-to-all(bf16[2,2,8,132,96]{4,1,3,0,2:T(2,128)(2,1)S(1)} %copy.88), channel_id=1, replica_groups=mesh['fsdp'=16,'tensor'=8] {'tensor'}, dimensions={2} | all-to-all | bytes 1622016 | tf_op jit(solution)/shard_map/all_to_all | solution.py:54
  29.6 0.7 copy.89
  30.3 0.0 copy-start.7
  30.4 2.1 copy.90
  32.5 7.8 %all-to-all-start.1 = ((bf16[2,16,1,132,96]{4,0,3,2,1:T(2,128)(2,1)}), bf16[2,16,1,132,96]{4,0,3,2,1:T(2,128)(2,1)S(1)}, u32[]{:S(2)}, u32[]{:S(2)}) async-start(bf16[2,16,1,132,96]{4,0,3,2,1:T(2,128)(2,1)} %copy.90), calls=%async_computation.1 | async-start | bytes 2162688 | tf_op jit(solution)/shard_map/all_to_all | solution.py:53
  40.2 0.0 copy-done.7
  40.2 0.6 fusion.7
  40.8 15.9 %all-to-all-done.1 = bf16[2,16,1,132,96]{4,0,3,2,1:T(2,128)(2,1)S(1)} async-done(((bf16[2,16,1,132,96]{4,0,3,2,1:T(2,128)(2,1)}), bf16[2,16,1,132,96]{4,0,3,2,1:T(2,128)(2,1)S(1)}, u32[]{:S(2)}, u32[]{:S(2)}) %all-to-all-start.1) | async-done | bytes 811040 | tf_op jit(solution)/shard_map/all_to_all | solution.py:53
  56.7 2.8 %fusion = f32[]{:T(128)} fusion(bf16[2,16,1,132,96]{4,0,3,2,1:T(2,128)(2,1)S(1)} %all-to-all-done.1), kind=kLoop, calls=%fused_computation.3 | loop fusion | flops 1216511 | bytes 811012 | tf_op jit(solution)/shard_map/reduce_sum | solution.py:62
  60.8 64.4 %psum.7 = f32[]{:T(128)} all-reduce(f32[]{:T(128)S(6)} %add.44), channel_id=1, replica_groups=mesh['fsdp'=16,'tensor'=8] {'fsdp','tensor'}, use_global_device_ids=true, to_apply=%region_2.0 | all-reduce | flops 1 | bytes 8 | tf_op jit(solution)/shard_map/psum | solution.py:62
  126.0 0.7 fusion.1
  126.7 0.4 copy.91
  127.1 2.3 mul.112
  129.4 6.5 %convert_bitcast_fusion = (bf16[2,1,1,132,1536]{4,3,0,2,1:T(8,128)(2,1)}, f32[2,132,1536]{2,1,0:T(8,128)}, f32[2,132,1536]{2,1,0:T(8,128)}, f32[2,132,1536]{2,1,0:T(8,128)S(1)}) fusion(f32[2,132,1536]{2,0,1:T(2,128)} %param.11, f32[2,132,1536]{2,1,0:T(8,128)} %mul.112, f32[2,132,1536]{2,0,1:T(2,128)} %param.12, f32[2,132,1536]{2,0,1:T(2,128)} %param.13), kind=kLoop, calls=%fused_computation.14 | loop fusion | flops 6488064 | bytes 12165120 | tf_op jit(solution)/shard_map/convert_element_type | solution.py:74
  135.9 3.5 %copy.95 = bf16[2,1,1,132,1536]{3,0,2,1,4:T(2,128)(2,1)S(1)} copy(bf16[2,1,1,132,1536]{4,3,0,2,1:T(8,128)(2,1)} %get-tuple-element.74) | data formatting | bytes 1622016 | tf_op jit(solution)/shard_map/convert_element_type | solution.py:74
  139.4 25.4 %all_to_all.81 = bf16[2,1,1,132,1536]{3,0,2,1,4:T(2,128)(2,1)} all-to-all(bf16[2,1,1,132,1536]{3,0,2,1,4:T(2,128)(2,1)S(1)} %copy.95), channel_id=1, replica_groups=mesh['fsdp'=16,'tensor'=8] {'fsdp'}, dimensions={4} | all-to-all | bytes 1622016 | tf_op jit(solution)/shard_map/all_to_all | solution.py:73
  164.9 3.5 %copy.112 = bf16[2,1,1,132,16,96]{5,4,3,0,2,1:T(8,128)(2,1)S(1)} copy(bf16[2,1,1,132,16,96]{3,0,5,4,2,1:T(2,128)(2,1)} %bitcast.41) | data formatting | bytes 1622016 | tf_op jit(solution)/shard_map/all_to_all | solution.py:73
  168.4 0.0 copy-start.2
  168.4 0.0 copy-start.3
  168.4 0.0 copy-start.4
  168.4 0.0 copy-start.5
  168.4 2.1 copy.97
  170.5 5.4 %all-to-all-start.3 = ((bf16[2,16,1,132,96]{4,0,3,2,1:T(2,128)(2,1)}), bf16[2,16,1,132,96]{4,0,3,2,1:T(2,128)(2,1)S(1)}, u32[]{:S(2)}, u32[]{:S(2)}) async-start(bf16[2,16,1,132,96]{4,0,3,2,1:T(2,128)(2,1)} %copy.97), calls=%async_computation.3 | async-start | bytes 2162688 | tf_op jit(solution)/shard_map/all_to_all | solution.py:72
  175.9 0.0 copy-done.2
  175.9 0.6 multiply_add_fusion
  176.5 14.8 %all-to-all-done.3 = bf16[2,16,1,132,96]{4,0,3,2,1:T(2,128)(2,1)S(1)} async-done(((bf16[2,16,1,132,96]{4,0,3,2,1:T(2,128)(2,1)}), bf16[2,16,1,132,96]{4,0,3,2,1:T(2,128)(2,1)S(1)}, u32[]{:S(2)}, u32[]{:S(2)}) %all-to-all-start.3) | async-done | bytes 811040 | tf_op jit(solution)/shard_map/all_to_all | solution.py:72
  191.4 0.7 stack.2
  192.1 0.3 copy-done.1
  192.4 4.3 %all-to-all-start.5 = ((bf16[128,2,24]{2,1,0:T(2,128)(2,1)}), bf16[128,2,24]{2,1,0:T(2,128)(2,1)S(1)}, u32[]{:S(2)}, u32[]{:S(2)}) async-start(bf16[128,2,24]{2,1,0:T(2,128)(2,1)} %stack.2), calls=%async_computation.5 | async-start | bytes 131072 | tf_op jit(solution)/shard_map/all_to_all | solution.py:91
  196.6 1.4 copy.98
  198.0 0.1 copy.129
  198.2 2.1 copy.102
  200.3 6.0 %all-to-all-done.5 = bf16[128,2,24]{2,1,0:T(2,128)(2,1)S(1)} async-done(((bf16[128,2,24]{2,1,0:T(2,128)(2,1)}), bf16[128,2,24]{2,1,0:T(2,128)(2,1)S(1)}, u32[]{:S(2)}, u32[]{:S(2)}) %all-to-all-start.5) | async-done | bytes 12320 | tf_op jit(solution)/shard_map/all_to_all | solution.py:91
  206.3 4.6 %all-to-all-start.4 = ((bf16[2,16,132,96]{3,0,2,1:T(2,128)(2,1)}), bf16[2,16,132,96]{3,0,2,1:T(2,128)(2,1)}, u32[]{:S(2)}, u32[]{:S(2)}) async-start(bf16[2,16,132,96]{3,0,2,1:T(2,128)(2,1)} %copy.102), calls=%async_computation.4 | async-start | bytes 2162688 | tf_op jit(solution)/shard_map/all_to_all | solution.py:84
  210.9 4.0 %copy.106 = f32[2,132,1536]{2,0,1:T(2,128)} copy(f32[2,132,1536]{2,1,0:T(8,128)} %get-tuple-element.75) | data formatting | bytes 3244032
  214.9 2.4 %copy.107 = f32[2,132,1536]{2,0,1:T(2,128)} copy(f32[2,132,1536]{2,1,0:T(8,128)S(1)} %copy-done) | data formatting | bytes 3244032
  217.3 2.4 %copy.108 = f32[2,132,1536]{2,0,1:T(2,128)} copy(f32[2,132,1536]{2,1,0:T(8,128)S(1)} %get-tuple-element.77) | data formatting | bytes 3244032
  219.7 0.7 reshape.59
  220.5 3.0 %copy.113 = bf16[2,2,8,1,132,96]{4,2,1,5,0,3:T(8,128)(2,1)S(1)} copy(bf16[2,2,8,1,132,96]{5,1,2,4,0,3:T(2,128)(2,1)S(1)} %bitcast.40) | data formatting | bytes 1622016
  223.4 2.9 %reshape.61 = bf16[2,2112,96]{1,2,0:T(8,128)(2,1)} reshape(bf16[2,2,8,1,132,96]{4,2,1,5,0,3:T(8,128)(2,1)S(1)} %copy.113) | data formatting | bytes 1622016
  226.3 0.9 all-to-all-done.4
  227.3 2.3 multiply_bitcast_fusion
  229.6 0.4 copy.103
  230.0 2.3 mul.125
  232.3 2.4 %fusion.3 = f32[2,132,1536]{2,1,0:T(8,128)S(1)} fusion(f32[2,132,1536]{2,1,0:T(8,128)} %mul.125, f32[2,132,1536]{2,0,1:T(2,128)} %param.14), kind=kLoop, calls=%fused_computation.8 | loop fusion | flops 811008 | bytes 4866048 | tf_op jit(solution)/shard_map/add | solution.py:88
  234.7 2.4 %copy.109 = f32[2,132,1536]{2,0,1:T(2,128)} copy(f32[2,132,1536]{2,1,0:T(8,128)S(1)} %fusion.3) | data formatting | bytes 3244032
  (10 shorter events, 0.0 us)
Async XLA Ops:
  30.3 9.9 %copy-start.7 = (bf16[2,24]{1,0:T(2,128)(2,1)S(1)}, bf16[2,24]{1,0:T(2,128)(2,1)}, u32[]{:S(2)}) copy-start(bf16[2,24]{1,0:T(2,128)(2,1)} %param.15) | copy-start | bytes 292
  32.5 24.2 %all-to-all-start.1 = ((bf16[2,16,1,132,96]{4,0,3,2,1:T(2,128)(2,1)}), bf16[2,16,1,132,96]{4,0,3,2,1:T(2,128)(2,1)S(1)}, u32[]{:S(2)}, u32[]{:S(2)}) async-start(bf16[2,16,1,132,96]{4,0,3,2,1:T(2,128)(2,1)} %copy.90), calls=%async_computation.1 | async-start | bytes 2162688 | tf_op jit(solution)/shard_map/all_to_all | solution.py:53
  168.4 7.5 %copy-start.2 = (f32[2,24]{1,0:T(2,128)S(1)}, f32[2,24]{1,0:T(2,128)}, u32[]{:S(2)}) copy-start(f32[2,24]{1,0:T(2,128)} %param.19) | copy-start | bytes 580
  168.4 7.5 %copy-start.3 = (f32[2,24]{1,0:T(2,128)S(1)}, f32[2,24]{1,0:T(2,128)}, u32[]{:S(2)}) copy-start(f32[2,24]{1,0:T(2,128)} %param.16) | copy-start | bytes 580
  168.4 7.5 %copy-start.4 = (f32[2,24]{1,0:T(2,128)S(1)}, f32[2,24]{1,0:T(2,128)}, u32[]{:S(2)}) copy-start(f32[2,24]{1,0:T(2,128)} %param.17) | copy-start | bytes 580
  168.4 7.5 %copy-start.5 = (f32[2,24]{1,0:T(2,128)S(1)}, f32[2,24]{1,0:T(2,128)}, u32[]{:S(2)}) copy-start(f32[2,24]{1,0:T(2,128)} %param.18) | copy-start | bytes 580
  170.5 20.8 %all-to-all-start.3 = ((bf16[2,16,1,132,96]{4,0,3,2,1:T(2,128)(2,1)}), bf16[2,16,1,132,96]{4,0,3,2,1:T(2,128)(2,1)S(1)}, u32[]{:S(2)}, u32[]{:S(2)}) async-start(bf16[2,16,1,132,96]{4,0,3,2,1:T(2,128)(2,1)} %copy.97), calls=%async_computation.3 | async-start | bytes 2162688 | tf_op jit(solution)/shard_map/all_to_all | solution.py:72
  176.5 21.6 %copy-start.6 = (f32[2,24]{1,0:T(2,128)}, f32[2,24]{1,0:T(2,128)S(1)}, u32[]{:S(2)}) copy-start(f32[2,24]{1,0:T(2,128)S(1)} %get-tuple-element.71) | copy-start | bytes 580
  191.4 1.0 copy-start.1
  192.4 13.9 %all-to-all-start.5 = ((bf16[128,2,24]{2,1,0:T(2,128)(2,1)}), bf16[128,2,24]{2,1,0:T(2,128)(2,1)S(1)}, u32[]{:S(2)}, u32[]{:S(2)}) async-start(bf16[128,2,24]{2,1,0:T(2,128)(2,1)} %stack.2), calls=%async_computation.5 | async-start | bytes 131072 | tf_op jit(solution)/shard_map/all_to_all | solution.py:91
  206.3 21.0 %all-to-all-start.4 = ((bf16[2,16,132,96]{3,0,2,1:T(2,128)(2,1)}), bf16[2,16,132,96]{3,0,2,1:T(2,128)(2,1)}, u32[]{:S(2)}, u32[]{:S(2)}) async-start(bf16[2,16,132,96]{3,0,2,1:T(2,128)(2,1)} %copy.102), calls=%async_computation.4 | async-start | bytes 2162688 | tf_op jit(solution)/shard_map/all_to_all | solution.py:84
  210.9 4.0 %copy-start = (f32[2,132,1536]{2,1,0:T(8,128)S(1)}, f32[2,132,1536]{2,1,0:T(8,128)}, u32[]{:S(2)}) copy-start(f32[2,132,1536]{2,1,0:T(8,128)} %get-tuple-element.76) | copy-start | bytes 4866052
